TPU v7x, 32 devices: a whole 2x2x4 slice. The times are simulated.
32 devices in a mesh: parts: 2 (over y), req: 4 (over z), tp: 2 (over x), sp: 2 (over core).
Axes of the slice: x: 2, y: 2, z: 4, core: 2. Of those that a mesh axis runs over, the one named last changes fastest.
Arguments:
- prompt_x: bfloat16 [1024, 16384], P(('parts', 'req', 'sp'), 'tp'), parts along dimension 0, may hold values from -600 to 600
- prompt_b: bfloat16 [1024, 8, 128], P(('parts', 'req', 'sp'), 'tp'), parts along dimension 0, may hold values from -0.5 to 0.5
- prompt_dt: float32 [1024, 256], P(('parts', 'req', 'sp'), 'tp'), parts along dimension 0, may hold values from 0.5 to 2
- cont_x: bfloat16 [8, 256, 16384], P(('parts', 'req'), 'sp', 'tp'), parts along dimension 0, may hold values from -6 to 6
- cont_bc: bfloat16 [8, 256, 2, 8, 128], P(('parts', 'req'), 'sp', None, 'tp'), parts along dimension 0, may hold values from -0.5 to 0.5
- cont_dt: float32 [8, 256, 256], P(('parts', 'req'), 'sp', 'tp'), parts along dimension 0, may hold values from 0.5 to 2
- decay_rate: float32 [256], P('tp'), may hold values from 0.0063476562 to 0.05
- skip_gain: float32 [256], P('tp'), may hold values from 0.5 to 1.5
- norm_gain: float32 [16384], P('tp'), may hold values from 0.25 to 1.75
- steer_vecs: float32 [7, 16384], P(None, 'tp'), may hold values from -3 to 3
- mult_table: float32 [9], replicated, may hold values from -3 to 3
- mult_idx: int32 [8], P(('parts', 'req')), parts along dimension 0, may hold values from 0 to 8
- behav_idx: int32 [8], P(('parts', 'req')), parts along dimension 0, may hold values from 0 to 6
Outputs:
- steered_out: bfloat16 [8, 256, 16384], P(('parts', 'req'), 'sp', 'tp'), parts along dimension 0
There are 2 independent parts, one for each index of `parts`. A program takes and returns all parts, laid end to end along the dimension named above; an argument that names none is the same for every part. Nothing has to cross between parts.
All inputs are finite; a program needn't handle non-finite values.
Results may differ from a plain program's by a relative error of at most 0.008.
Values sent between devices are 32-bit elements; how exact they have to be, the bound alone decides.
A program may use at most 320 MiB of HBM per device.

v0:
```python
import jax
import jax.numpy as jnp
from jax import lax
from jax.sharding import PartitionSpec as P

HEADS = 256
HEAD_DIM = 64


def block_state(rows_x, rows_b, rows_dt, decay_rate, groups):
    length = rows_x.shape[0]
    head_count = decay_rate.shape[0]
    per_group = head_count // groups
    head_size = rows_x.shape[1] // head_count
    cumulative = jnp.cumsum(-decay_rate[None, :] * rows_dt, axis=0)
    block_total = cumulative[-1]
    weight = jnp.exp(block_total[None, :] - cumulative) * rows_dt
    scaled = (
        rows_x.astype(jnp.float32).reshape(length, head_count, head_size) * weight[:, :, None]
    ).astype(jnp.bfloat16)
    scaled = scaled.reshape(length, groups, per_group, head_size)
    local_state = jnp.einsum("tgqp,tgn->gqpn", scaled, rows_b, preferred_element_type=jnp.float32)
    carried = jnp.einsum(
        "tgq,tgn->gqn",
        weight.reshape(length, groups, per_group),
        rows_b.astype(jnp.float32),
        precision=lax.Precision.HIGHEST,
    )
    return (
        block_total,
        local_state.reshape(head_count, head_size, -1),
        carried.reshape(head_count, -1),
        cumulative,
    )


def intra_block(steered, bmat, cmat, rows_dt, cumulative, groups):
    length = steered.shape[0]
    head_count = rows_dt.shape[1]
    per_group = head_count // groups
    head_size = steered.shape[1] // head_count
    products = jnp.einsum("tgn,sgn->gts", cmat, bmat, preferred_element_type=jnp.float32)
    lower_mask = lax.broadcasted_iota(jnp.int32, (length, length), 0) >= lax.broadcasted_iota(
        jnp.int32, (length, length), 1
    )
    row_factor = jnp.exp(cumulative).reshape(length, groups, per_group).transpose(1, 2, 0)
    col_factor = (
        (jnp.exp(-cumulative) * rows_dt).reshape(length, groups, per_group).transpose(1, 2, 0)
    )
    full = products[:, None, :, :] * row_factor[:, :, :, None] * col_factor[:, :, None, :]
    mixing = jnp.where(lower_mask[None, None], full, 0.0).astype(jnp.bfloat16)
    input_groups = steered.reshape(length, groups, per_group, head_size)
    outputs = jnp.einsum(
        "gqts,sgqp->tgqp", mixing, input_groups, preferred_element_type=jnp.float32
    )
    return outputs.reshape(length, head_count, head_size)


def local(
    prompt_x,
    prompt_b,
    prompt_dt,
    cont_x,
    cont_bc,
    cont_dt,
    decay_rate,
    skip_gain,
    norm_gain,
    steer_vecs,
    mult_table,
    mult_idx,
    behav_idx,
):
    groups = prompt_b.shape[1]
    head_count = decay_rate.shape[0]
    per_group = head_count // groups
    head_size = norm_gain.shape[0] // head_count
    prompt_total, prompt_state, prompt_carry, unused = block_state(
        prompt_x, prompt_b, prompt_dt, decay_rate, groups
    )
    place = lax.axis_index(("req", "sp"))
    totals = lax.all_gather(prompt_total, ("req", "sp"))
    later = lax.broadcasted_iota(jnp.int32, totals.shape, 0) > place
    remaining = jnp.exp(jnp.sum(jnp.where(later, totals, 0.0), axis=0))
    prefix_state, prefix_carry = lax.psum(
        (remaining[:, None, None] * prompt_state, remaining[:, None] * prompt_carry), ("req", "sp")
    )
    picked = lax.broadcasted_iota(jnp.int32, mult_table.shape, 0) == mult_idx[0]
    multiplier = jnp.sum(jnp.where(picked, mult_table, 0.0))
    choose = lax.broadcasted_iota(jnp.int32, (steer_vecs.shape[0], 1), 0) == behav_idx[0]
    vector = jnp.sum(jnp.where(choose, steer_vecs, 0.0), axis=0)
    steered = (cont_x[0].astype(jnp.float32) + multiplier * vector[None, :]).astype(jnp.bfloat16)
    bmat = cont_bc[0, :, 0]
    cmat = cont_bc[0, :, 1]
    rows_dt = cont_dt[0]
    length = steered.shape[0]
    block_total, local_state, carried, cumulative = block_state(
        steered, bmat, rows_dt, decay_rate, groups
    )
    before_total, before_state = lax.ppermute((block_total, local_state), "sp", [(0, 1)])
    inner = intra_block(steered, bmat, cmat, rows_dt, cumulative, groups)
    start_state = (
        prefix_state
        + multiplier * vector.reshape(head_count, head_size)[:, :, None] * prefix_carry[:, None, :]
    )
    incoming = jnp.exp(before_total)[:, None, None] * start_state + before_state
    incoming_round = incoming.astype(jnp.bfloat16).reshape(groups, per_group, head_size, -1)
    from_state = jnp.einsum(
        "tgn,gqpn->tgqp", cmat, incoming_round, preferred_element_type=jnp.float32
    ).reshape(length, head_count, head_size)
    skipped = skip_gain[None, :, None] * steered.astype(jnp.float32).reshape(
        length, head_count, head_size
    )
    mixed = (inner + jnp.exp(cumulative)[:, :, None] * from_state + skipped).reshape(
        length, head_count * head_size
    )
    squares = jnp.sum(mixed * mixed, axis=1)
    total_squares = lax.psum(squares, "tp")
    meansq = total_squares / (HEADS * HEAD_DIM)
    return (mixed * lax.rsqrt(meansq + 1e-05)[:, None] * norm_gain[None, :]).astype(jnp.bfloat16)[
        None
    ]


def solution(mesh):
    return jax.shard_map(
        local,
        mesh=mesh,
        in_specs=(
            P(("parts", "req", "sp"), "tp"),
            P(("parts", "req", "sp"), "tp", None),
            P(("parts", "req", "sp"), "tp"),
            P(("parts", "req"), "sp", "tp"),
            P(("parts", "req"), "sp", None, "tp", None),
            P(("parts", "req"), "sp", "tp"),
            P("tp"),
            P("tp"),
            P("tp"),
            P(None, "tp"),
            P(),
            P(("parts", "req")),
            P(("parts", "req")),
        ),
        out_specs=P(("parts", "req"), "sp", "tp"),
        check_vma=False,
    )
```

profile of v0, /device:TPU:0, one launch (start us, length us, event | category | flops | bytes accessed | tf_op | source)
XLA Modules:
  0.0 185.2 jit_solution(16064497047261371977)
XLA Ops:
  6.5 0.7 neg.9
  7.2 0.8 bitcast_multiply_fusion.4
  8.1 0.2 reduce_window_sum.24
  8.3 0.7 copy.42
  9.0 1.6 copy.43
  10.6 0.1 sub.27
  11.9 1.1 select_reduce_fusion
  13.1 1.3 fusion.34
  14.3 0.6 broadcast_multiply_fusion.1
  15.0 0.1 mul.204
  15.1 0.5 copy-done.5
  15.6 3.2 %copy.39 = bf16[1,128,8192]{1,2,0:T(8,128)(2,1)S(1)} copy(bf16[1,128,8192]{2,1,0:T(8,128)(2,1)} %param.16) | data formatting | bytes 4194304 | tf_op args[3]
  18.8 0.0 copy-start.8
  18.8 0.0 copy-start.2
  18.8 1.2 fusion.36
  20.0 1.6 fusion.37
  21.6 2.8 %fusion.17 = f32[4,32,64,128]{3,2,1,0:T(8,128)} fusion(f32[128,4,32]{0,2,1:T(8,128)S(1)} %get-tuple-element.14, bf16[1,128,1,4,128]{4,3,2,1,0:T(4,128)(2,1)S(1)} %get-tuple-element.8, f32[4,32,64]{2,1,0:T(8,128)S(1)} %mul.204, bf16[128,4,32,64]{0,3,2,1:T(8,128)(2,1)S(1)} %bitcast.77), kind=kOutput, calls=%fused_computation.27 | convolution fusion | flops 274726912 | bytes 6520832 | tf_op jit(solution)/shard_map/tgqp,tgn->gqpn/dot_general | solution.py:22
  24.3 4.3 %collective-permute-start.1 = (f32[128,64,128]{2,1,0:T(8,128)}, f32[128,64,128]{2,1,0:T(8,128)}, u32[]{:S(2)}, u32[]{:S(2)}) collective-permute-start(f32[128,64,128]{2,1,0:T(8,128)} %bitcast.24), channel_id=1, source_target_pairs={{0,1},{2,3},{4,5},{6,7},{8,9},{10,11},{12,13},{14,15},{16,17},{18,... | collective-permute-start | bytes 12582920 | tf_op jit(solution)/shard_map/ppermute | solution.py:100
  28.7 0.6 broadcast_multiply_fusion
  29.3 1.4 reduce_window_sum.26
  30.7 0.7 slice_bitcast_fusion.1
  31.4 1.4 exponential_multiply_fusion.1
  32.8 1.5 copy.45
  34.2 2.4 %copy.53 = f32[64,8192]{0,1:T(8,128)} copy(bf16[64,8192]{1,0:T(8,128)(2,1)S(1)} %copy-done.2) | data formatting | bytes 3145728 | tf_op jit(solution)/shard_map/reshape | solution.py:19
  36.6 12.7 %all-gather = f32[8,1,128]{2,1,0:T(1,128)S(1)} all-gather(f32[1,1,128]{2,1,0:T(1,128)S(1)} %get-tuple-element.17), channel_id=1, replica_groups=mesh['parts'=2,'req'=4,'tp'=2,'sp'=2] {'req','sp'}, dimensions={0}, use_global_device_ids=true | all-gather | bytes 4608 | tf_op jit(solution)/shard_map/all_gather | solution.py:82
  49.4 0.1 select_reduce_fusion.1
  49.5 1.0 fusion.32
  50.5 0.7 bitcast_multiply_fusion.3
  51.2 2.9 %fusion.16 = f32[4,32,64,128]{3,2,1,0:T(8,128)S(1)} fusion(f32[64,4,32,64]{0,3,2,1:T(8,128)} %bitcast.80, f32[64,4,32]{0,2,1:T(8,128)} %bitcast.85, bf16[64,4,128,1]{2,1,0,3:T(4,128)(2,1)S(1)} %bitcast.76), kind=kOutput, calls=%fused_computation.26 | convolution fusion | flops 135266304 | bytes 6389760 | tf_op jit(solution)/shard_map/tgqp,tgn->gqpn/dot_general | solution.py:22
  54.1 2.3 %bitcast_multiply_fusion.1 = f32[128,64,128]{2,1,0:T(8,128)} fusion(f32[4,32,64,128]{3,2,1,0:T(8,128)S(1)} %fusion.16, f32[128]{0:T(128)S(1)} %exp.44), kind=kLoop, calls=%fused_computation.10 | loop fusion | flops 1048576 | bytes 8389120 | tf_op jit(solution)/shard_map/mul | solution.py:86
  56.3 0.0 all-reduce.3.cloned.1.call-update
  56.4 2.3 %collective-permute-start = (f32[128]{0:T(128)S(1)}, f32[128]{0:T(128)S(1)}, u32[]{:S(2)}, u32[]{:S(2)}) collective-permute-start(f32[128]{0:T(128)S(1)} %get-tuple-element.15), channel_id=1, source_target_pairs={{0,1},{2,3},{4,5},{6,7},{8,9},{10,11},{12,13},{14,15},{16,17},{18,... | collective-permute-start | bytes 1544 | tf_op jit(solution)/shard_map/ppermute | solution.py:100
  58.7 0.2 fusion.24
  59.0 0.0 copy-start.12
  59.0 6.3 %fusion.4 = f32[4,32,64,128]{3,2,1,0:T(8,128)} fusion(f32[4,32,128]{2,1,0:T(8,128)S(1)} %copy-done.10, f32[4,32,128]{2,1,0:T(8,128)S(1)} %copy-done.9, f32[4,128,128]{2,1,0:T(8,128)S(1)} %fusion.24, pred[128,128]{1,0:T(8,128)(4,1)S(1)} %iota_compare_fusion, f32[4,32,64]{2,1,0:T(8,128)S(1)} %mul.204, bf16[128,4,32,64]{0,3,2,1:T(8,128)(2,1)S(1)} %bitcast.78), kind=kOutput, calls=%fused_computation.7 | convolution fusion | flops 279969792 | bytes 6733824 | tf_op jit(solution)/shard_map/gqts,sgqp->tgqp/dot_general | solution.py:53
  65.3 0.1 mul.225
  65.4 0.1 mul.242
  65.5 0.1 copy.44
  65.6 0.1 mul.236
  65.7 0.1 mul.237
  65.8 0.0 collective-permute-done
  65.8 87.1 %all-reduce.3.cloned.1.call-done = (f32[128,64,128]{2,1,0:T(8,128)}, f32[128,128]{1,0:T(8,128)}) async-done(((f32[128,64,128]{2,1,0:T(8,128)}, f32[128,128]{1,0:T(8,128)}), (f32[128,64,128]{2,1,0:T(8,128)}, f32[128,128]{1,0:T(8,128)})) %all-reduce.3.cloned.1.call-update) | async-done | bytes 4259856 | tf_op jit(solution)/shard_map/psum | solution.py:85
  152.9 4.4 %add_convert_fusion.1 = bf16[128,64,128]{2,1,0:T(8,128)(2,1)S(1)} fusion(f32[128,64,128]{2,1,0:T(8,128)} %collective-permute-done.1, f32[128,64,128]{2,1,0:T(8,128)} %get-tuple-element.5, f32[128,128]{1,0:T(8,128)} %get-tuple-element.6, f32[128,64]{1,0:T(8,128)S(1)} %mul.225, f32[128]{0:T(128)S(1)} %exp.43), kind=kLoop, calls=%fused_computation.18 | loop fusion | flops 5242880 | bytes 10584576 | tf_op jit(solution)/shard_map/convert_element_type | solution.py:107
  157.3 0.2 copy-done.1
  157.6 3.2 %fusion.3 = (f32[128]{0:T(128)S(1)}, f32[4,32,64,128]{3,2,1,0:T(8,128)}) fusion(f32[4,32,64,128]{3,2,1,0:T(8,128)S(1)} %copy-done.1, f32[4,32]{1,0:T(4,128)S(1)} %mul.242, f32[128,4,32]{0,2,1:T(8,128)S(1)} %copy-done.7, bf16[4,32,64,128]{3,2,1,0:T(8,128)(2,1)S(1)} %bitcast.83, bf16[1,128,1,4,128]{4,3,2,1,0:T(4,128)(2,1)S(1)} %get-tuple-element.7, ...), kind=kOutput, calls=%fused_computation.6 | convolution fusion | flops 278921088 | bytes 12813312 | tf_op jit(solution)/shard_map/tgn,gqpn->tgqp/dot_general | solution.py:108
  160.8 4.9 %psum.23 = f32[128]{0:T(128)S(1)} all-reduce(f32[128]{0:T(128)S(1)} %get-tuple-element.19), channel_id=1, replica_groups=mesh['parts'=2,'req'=4,'tp'=2,'sp'=2] {'tp'}, use_global_device_ids=true, to_apply=%region_8.9 | all-reduce | flops 128 | bytes 1024 | tf_op jit(solution)/shard_map/psum | solution.py:118
  165.7 8.5 %fusion.10 = bf16[1,128,8192]{1,2,0:T(8,128)(2,1)} fusion(f32[1,128,8192]{1,2,0:T(8,128)} %bitcast.81, f32[1,128,8192]{1,2,0:T(8,128)} %bitcast.82, f32[8192]{0:T(1024)S(1)} %copy-done.11, f32[128]{0:T(128)S(1)} %add_rsqrt_fusion, f32[8192]{0:T(1024)S(1)} %copy-done.6, f32[8192]{0:T(1024)S(1)} %mul.237, f32[128,128]{0,1:T(8,128)S(1)} %copy.44, ...), kind=kLoop, calls=%fused_computation.16 | loop fusion | flops 11534336 | bytes 12747264 | tf_op jit(solution)/shard_map/convert_element_type | solution.py:120
  174.3 4.1 %copy.49 = bf16[1,128,8192]{2,1,0:T(8,128)(2,1)} copy(bf16[1,128,8192]{1,2,0:T(8,128)(2,1)} %fusion.10) | data formatting | bytes 4194304 | tf_op jit(solution)/shard_map/convert_element_type | solution.py:120
  (31 shorter events, 0.1 us)
Async XLA Ops:
  6.5 42.9 %copy-start = (bf16[64,4,128]{2,1,0:T(4,128)(2,1)S(1)}, bf16[64,4,128]{2,1,0:T(4,128)(2,1)}, u32[]{:S(2)}) copy-start(bf16[64,4,128]{2,1,0:T(4,128)(2,1)} %param.14) | copy-start | bytes 196612
  6.5 146.3 %all-reduce.3.cloned.1.call-start = ((), (), s32[]{:S(2)}) async-start(), calls=%async_computation | async-start | bytes 8519680 | tf_op jit(solution)/shard_map/psum | solution.py:85
  8.2 6.7 %copy-start.3 = (f32[128,128]{1,0:T(8,128)}, f32[128,128]{1,0:T(8,128)S(1)}, u32[]{:S(2)}) copy-start(f32[128,128]{1,0:T(8,128)S(1)} %reduce_window_sum.24) | copy-start | bytes 196612
  15.0 0.6 copy-start.5
  18.8 9.8 %copy-start.8 = (f32[64,128]{1,0:T(8,128)S(1)}, f32[64,128]{1,0:T(8,128)}, u32[]{:S(2)}) copy-start(f32[64,128]{1,0:T(8,128)} %param.15) | copy-start | bytes 98308
  18.8 15.4 %copy-start.2 = (bf16[64,8192]{1,0:T(8,128)(2,1)S(1)}, bf16[64,8192]{1,0:T(8,128)(2,1)}, u32[]{:S(2)}) copy-start(bf16[64,8192]{1,0:T(8,128)(2,1)} %param.13) | copy-start | bytes 3145732
  24.3 128.5 %collective-permute-start.1 = (f32[128,64,128]{2,1,0:T(8,128)}, f32[128,64,128]{2,1,0:T(8,128)}, u32[]{:S(2)}, u32[]{:S(2)}) collective-permute-start(f32[128,64,128]{2,1,0:T(8,128)} %bitcast.24), channel_id=1, source_target_pairs={{0,1},{2,3},{4,5},{6,7},{8,9},{10,11},{12,13},{14,15},{16,17},{18,... | collective-permute-start | bytes 12582920 | tf_op jit(solution)/shard_map/ppermute | solution.py:100
  56.3 2.6 %copy-start.9 = (f32[4,32,128]{2,1,0:T(8,128)S(1)}, f32[4,32,128]{2,1,0:T(8,128)}, u32[]{:S(2)}) copy-start(f32[4,32,128]{2,1,0:T(8,128)} %get-tuple-element.12) | copy-start | bytes 196612
  56.3 2.6 %copy-start.10 = (f32[4,32,128]{2,1,0:T(8,128)S(1)}, f32[4,32,128]{2,1,0:T(8,128)}, u32[]{:S(2)}) copy-start(f32[4,32,128]{2,1,0:T(8,128)} %get-tuple-element.13) | copy-start | bytes 196612
  56.4 9.4 %collective-permute-start = (f32[128]{0:T(128)S(1)}, f32[128]{0:T(128)S(1)}, u32[]{:S(2)}, u32[]{:S(2)}) collective-permute-start(f32[128]{0:T(128)S(1)} %get-tuple-element.15), channel_id=1, source_target_pairs={{0,1},{2,3},{4,5},{6,7},{8,9},{10,11},{12,13},{14,15},{16,17},{18,... | collective-permute-start | bytes 1544 | tf_op jit(solution)/shard_map/ppermute | solution.py:100
  59.0 6.3 %copy-start.6 = (f32[8192]{0:T(1024)S(1)}, f32[8192]{0:T(1024)}, u32[]{:S(2)}) copy-start(f32[8192]{0:T(1024)} %copy-done.5) | copy-start | bytes 98308
  59.0 6.4 %copy-start.4 = (f32[128,128]{1,0:T(8,128)S(1)}, f32[128,128]{1,0:T(8,128)}, u32[]{:S(2)}) copy-start(f32[128,128]{1,0:T(8,128)} %copy-done.3) | copy-start | bytes 196612
  59.0 6.4 %copy-start.12 = (f32[128]{0:T(128)S(1)}, f32[128]{0:T(128)}, u32[]{:S(2)}) copy-start(f32[128]{0:T(128)} %param.20) | copy-start | bytes 1540
  152.9 4.7 %copy-start.1 = (f32[4,32,64,128]{3,2,1,0:T(8,128)S(1)}, f32[4,32,64,128]{3,2,1,0:T(8,128)}, u32[]{:S(2)}) copy-start(f32[4,32,64,128]{3,2,1,0:T(8,128)} %fusion.4) | copy-start | bytes 12582916
  152.9 4.7 %copy-start.7 = (f32[128,4,32]{0,2,1:T(8,128)S(1)}, f32[128,4,32]{0,2,1:T(8,128)}, u32[]{:S(2)}) copy-start(f32[128,4,32]{0,2,1:T(8,128)} %get-tuple-element.11) | copy-start | bytes 196612
  157.6 8.2 %copy-start.11 = (f32[8192]{0:T(1024)S(1)}, f32[8192]{0:T(1024)}, u32[]{:S(2)}) copy-start(f32[8192]{0:T(1024)} %param.21) | copy-start | bytes 98308
Sparse Core Ops, SparseCore 0:
  56.5 96.3 all-reduce.2
where the time goes:
time: 186 us; the launch traced here: 185 us
  waiting for transfers between devices  87.1 us (47%)
  other arithmetic  25.8 us (14%)
  blocking collectives  17.7 us (10%)
  local copies, waits for them, and re-layouts  16.7 us (9%)
  matrix products  16.4 us (9%)
  between operations  14.9 us (8%)
  starting transfers between devices  6.66 us (4%)
    psum x1, waiting for transfers between devices, local(): lax.psum((remaining[:, None, None] * prompt_state, remaining[:, None] * p...  87.1 us
    all_gather x1, blocking collectives, local(): totals = lax.all_gather(prompt_total, ('req', 'sp'))  12.7 us
    convert_element_type x1, other arithmetic, local(): (mixed * lax.rsqrt(meansq + 1e-05)[:, None] * norm_gain[None, :]).astype(...  8.54 us
    ppermute x2, starting transfers between devices, local(): lax.ppermute((block_total, local_state), 'sp', [(0, 1)])  6.66 us
    dot_general x1, matrix products, intra_block(): jnp.einsum('gqts,sgqp->tgqp', mixing, input_groups, preferred_element_typ...  6.31 us
    unnamed x29, local copies, waits for them, and re-layouts  6.24 us
    dot_general x2, matrix products, block_state(): jnp.einsum('tgqp,tgn->gqpn', scaled, rows_b, preferred_element_type=jnp.f...  5.64 us
    psum x1, blocking collectives, local(): total_squares = lax.psum(squares, 'tp')  4.92 us
  transfers between devices with their start and end apart: 3, of which 1 were waited for; matrix products, arithmetic and copies ran while one was open for 12% of the time, Pallas kernels for 0%

commit v1 on v0

--- a/solution.py
+++ b/solution.py
@@ -82,8 +82,14 @@
     totals = lax.all_gather(prompt_total, ("req", "sp"))
     later = lax.broadcasted_iota(jnp.int32, totals.shape, 0) > place
     remaining = jnp.exp(jnp.sum(jnp.where(later, totals, 0.0), axis=0))
-    prefix_state, prefix_carry = lax.psum(
-        (remaining[:, None, None] * prompt_state, remaining[:, None] * prompt_carry), ("req", "sp")
+
+    def recast_the_meshes(s0, comm_axis, axis_key):
+        for dd in (comm_axis, axis_key):
+            s0 = lax.psum(s0, dd)
+        return s0
+
+    prefix_state, prefix_carry = recast_the_meshes(
+        (remaining[:, None, None] * prompt_state, remaining[:, None] * prompt_carry), "sp", "req"
     )
     picked = lax.broadcasted_iota(jnp.int32, mult_table.shape, 0) == mult_idx[0]
     multiplier = jnp.sum(jnp.where(picked, mult_table, 0.0))

time: 186 us -> 253 us (1.36)
  waiting for transfers between devices: 87.1 us -> 166 us
  other arithmetic: 25.8 us -> 20.1 us
  local copies, waits for them, and re-layouts: 16.7 us -> 12.1 us
    psum x1 -> x2, waiting for transfers between devices: 87.1 us -> 166 us  [recast_the_meshes(): s0 = lax.psum(s0, dd)]
    unnamed x29 -> x19, local copies, waits for them, and re-layouts: 6.24 us -> 3.81 us
  transfers between devices with their start and end apart: 3 -> 4, of which waited for: 1 -> 2; matrix products, arithmetic and copies ran while one was open for 12% -> 6% of each run, Pallas kernels for 0% -> 0%
where the time goes in v1:
time: 253 us; the launch traced here: 252 us
  waiting for transfers between devices  166 us (66%)
  other arithmetic  20.1 us (8%)
  blocking collectives  18.3 us (7%)
  matrix products  15.6 us (6%)
  between operations  14.9 us (6%)
  local copies, waits for them, and re-layouts  12.1 us (5%)
  starting transfers between devices  5.39 us (2%)
    psum x2, waiting for transfers between devices, recast_the_meshes(): s0 = lax.psum(s0, dd)  166 us
    all_gather x1, blocking collectives, local(): totals = lax.all_gather(prompt_total, ('req', 'sp'))  13.4 us
    convert_element_type x1, other arithmetic, local(): (mixed * lax.rsqrt(meansq + 1e-05)[:, None] * norm_gain[None, :]).astype(...  8.57 us
    dot_general x1, matrix products, intra_block(): jnp.einsum('gqts,sgqp->tgqp', mixing, input_groups, preferred_element_typ...  6.32 us
    dot_general x2, matrix products, block_state(): jnp.einsum('tgqp,tgn->gqpn', scaled, rows_b, preferred_element_type=jnp.f...  5.66 us
    ppermute x2, starting transfers between devices, local(): lax.ppermute((block_total, local_state), 'sp', [(0, 1)])  5.35 us
  transfers between devices with their start and end apart: 4, of which 2 were waited for; matrix products, arithmetic and copies ran while one was open for 6% of the time, Pallas kernels for 0%

profile of v1, /device:TPU:0, one launch (start us, length us, event | category | flops | bytes accessed | tf_op | source)
XLA Modules:
  0.0 252.3 jit_solution(136720457371602978)
XLA Ops:
  6.5 0.7 neg.9
  7.2 0.8 broadcast_multiply_fusion
  8.0 0.1 reduce_window_sum.26
  8.1 0.8 exponential_multiply_fusion.1
  8.9 0.1 copy.45
  9.0 3.3 %copy.53 = f32[64,8192]{0,1:T(8,128)} copy(bf16[64,8192]{1,0:T(8,128)(2,1)} %param.13) | data formatting | bytes 3145728 | tf_op jit(solution)/shard_map/reshape | solution.py:19
  12.3 13.4 %all-gather = f32[8,1,128]{2,1,0:T(1,128)S(1)} all-gather(f32[1,1,128]{2,1,0:T(1,128)S(1)} %get-tuple-element.19), channel_id=1, replica_groups=mesh['parts'=2,'req'=4,'tp'=2,'sp'=2] {'req','sp'}, dimensions={0}, use_global_device_ids=true | all-gather | bytes 4608 | tf_op jit(solution)/shard_map/all_gather | solution.py:82
  25.7 0.1 select_reduce_fusion.1
  25.8 0.2 fusion.32
  25.9 2.9 %fusion.16 = f32[4,32,64,128]{3,2,1,0:T(8,128)S(1)} fusion(f32[64,4,32,64]{0,3,2,1:T(8,128)} %bitcast.80, f32[64,4,32]{0,2,1:T(8,128)S(1)} %bitcast.85, bf16[64,4,128,1]{2,1,0,3:T(4,128)(2,1)S(1)} %bitcast.76), kind=kOutput, calls=%fused_computation.26 | convolution fusion | flops 135266304 | bytes 6389760 | tf_op jit(solution)/shard_map/tgqp,tgn->gqpn/dot_general | solution.py:22
  28.8 2.3 bitcast_multiply_fusion.1
  31.1 0.7 bitcast_multiply_fusion.3
  31.8 0.0 all-reduce.7.cloned.1.call-update
  31.9 0.0 all-reduce.5.cloned.1.call-start
  31.9 0.0 copy-done.4
  32.0 0.1 copy.43
  32.1 0.2 reduce_window_sum.24
  32.2 0.1 copy.42
  32.4 0.1 sub.27
  33.8 0.6 fusion.34
  34.4 0.1 select_reduce_fusion
  34.5 0.6 broadcast_multiply_fusion.1
  35.2 0.1 mul.204
  35.3 3.4 %copy.39 = bf16[1,128,8192]{1,2,0:T(8,128)(2,1)S(1)} copy(bf16[1,128,8192]{2,1,0:T(8,128)(2,1)} %param.16) | data formatting | bytes 4194304 | tf_op args[3]
  38.7 0.1 fusion.36
  38.8 0.1 fusion.37
  38.9 20.0 %all-reduce.7.cloned.1.call-done = (f32[128,64,128]{2,1,0:T(8,128)}, f32[128,128]{1,0:T(8,128)}) async-done(((f32[128,64,128]{2,1,0:T(8,128)}, f32[128,128]{1,0:T(8,128)}), (f32[128,64,128]{2,1,0:T(8,128)}, f32[128,128]{1,0:T(8,128)})) %all-reduce.7.cloned.1.call-update) | async-done | bytes 4259856 | tf_op jit(solution)/shard_map/psum | solution.py:88
  58.9 0.0 all-reduce.5.cloned.1.call-update
  58.9 2.8 %fusion.17 = f32[4,32,64,128]{3,2,1,0:T(8,128)} fusion(f32[128,4,32]{0,2,1:T(8,128)S(1)} %get-tuple-element.16, bf16[1,128,1,4,128]{4,3,2,1,0:T(4,128)(2,1)S(1)} %get-tuple-element.10, f32[4,32,64]{2,1,0:T(8,128)S(1)} %mul.204, bf16[128,4,32,64]{0,3,2,1:T(8,128)(2,1)S(1)} %bitcast.77), kind=kOutput, calls=%fused_computation.27 | convolution fusion | flops 274726912 | bytes 6520832 | tf_op jit(solution)/shard_map/tgqp,tgn->gqpn/dot_general | solution.py:22
  61.7 4.1 %collective-permute-start.1 = (f32[128,64,128]{2,1,0:T(8,128)}, f32[128,64,128]{2,1,0:T(8,128)}, u32[]{:S(2)}, u32[]{:S(2)}) collective-permute-start(f32[128,64,128]{2,1,0:T(8,128)} %bitcast.24), channel_id=1, source_target_pairs={{0,1},{2,3},{4,5},{6,7},{8,9},{10,11},{12,13},{14,15},{16,17},{18,... | collective-permute-start | bytes 12582920 | tf_op jit(solution)/shard_map/ppermute | solution.py:106
  65.8 1.3 collective-permute-start
  67.1 0.2 fusion.24
  67.3 0.0 copy-start.6
  67.3 6.3 %fusion.4 = f32[4,32,64,128]{3,2,1,0:T(8,128)} fusion(f32[4,32,128]{2,1,0:T(8,128)S(1)} %get-tuple-element.15, f32[4,32,128]{2,1,0:T(8,128)S(1)} %get-tuple-element.14, f32[4,128,128]{2,1,0:T(8,128)S(1)} %fusion.24, pred[128,128]{1,0:T(8,128)(4,1)S(1)} %iota_compare_fusion, f32[4,32,64]{2,1,0:T(8,128)S(1)} %mul.204, bf16[128,4,32,64]{0,3,2,1:T(8,128)(2,1)S(1)} %bitcast.78), kind=kOutput, calls=%fused_computation.7 | convolution fusion | flops 279969792 | bytes 6733824 | tf_op jit(solution)/shard_map/gqts,sgqp->tgqp/dot_general | solution.py:53
  73.6 0.1 mul.225
  73.7 0.1 mul.242
  73.8 0.1 copy.44
  73.9 0.1 mul.236
  74.0 0.1 mul.237
  74.1 0.0 collective-permute-done
  74.1 0.0 collective-permute-done.1
  74.1 145.9 %all-reduce.5.cloned.1.call-done = (f32[128,64,128]{2,1,0:T(8,128)}, f32[128,128]{1,0:T(8,128)}) async-done(((f32[128,64,128]{2,1,0:T(8,128)}, f32[128,128]{1,0:T(8,128)}), (f32[128,64,128]{2,1,0:T(8,128)}, f32[128,128]{1,0:T(8,128)})) %all-reduce.5.cloned.1.call-update) | async-done | bytes 4259856 | tf_op jit(solution)/shard_map/psum | solution.py:88
  220.0 4.4 %add_convert_fusion.1 = bf16[128,64,128]{2,1,0:T(8,128)(2,1)S(1)} fusion(f32[128,64,128]{2,1,0:T(8,128)} %collective-permute-done.1, f32[128,64,128]{2,1,0:T(8,128)} %get-tuple-element.5, f32[128,128]{1,0:T(8,128)} %get-tuple-element.6, f32[128,64]{1,0:T(8,128)S(1)} %mul.225, f32[128]{0:T(128)S(1)} %exp.43), kind=kLoop, calls=%fused_computation.18 | loop fusion | flops 5242880 | bytes 10584576 | tf_op jit(solution)/shard_map/convert_element_type | solution.py:113
  224.4 0.2 copy-done.1
  224.7 3.2 %fusion.3 = (f32[128]{0:T(128)S(1)}, f32[4,32,64,128]{3,2,1,0:T(8,128)}) fusion(f32[4,32,64,128]{3,2,1,0:T(8,128)S(1)} %copy-done.1, f32[4,32]{1,0:T(4,128)S(1)} %mul.242, f32[128,4,32]{0,2,1:T(8,128)S(1)} %get-tuple-element.13, bf16[4,32,64,128]{3,2,1,0:T(8,128)(2,1)S(1)} %bitcast.83, bf16[1,128,1,4,128]{4,3,2,1,0:T(4,128)(2,1)S(1)} %get-tuple-element.9, ...), kind=kOutput, calls=%fused_computation.6 | convolution fusion | flops 278921088 | bytes 12813312 | tf_op jit(solution)/shard_map/tgn,gqpn->tgqp/dot_general | solution.py:114
  227.9 4.9 %psum.39 = f32[128]{0:T(128)S(1)} all-reduce(f32[128]{0:T(128)S(1)} %get-tuple-element.21), channel_id=1, replica_groups=mesh['parts'=2,'req'=4,'tp'=2,'sp'=2] {'tp'}, use_global_device_ids=true, to_apply=%region_10.11 | all-reduce | flops 128 | bytes 1024 | tf_op jit(solution)/shard_map/psum | solution.py:124
  232.8 8.6 %fusion.10 = bf16[1,128,8192]{1,2,0:T(8,128)(2,1)} fusion(f32[1,128,8192]{1,2,0:T(8,128)} %bitcast.81, f32[1,128,8192]{1,2,0:T(8,128)} %bitcast.82, f32[8192]{0:T(1024)S(1)} %copy-done.5, f32[128]{0:T(128)S(1)} %add_rsqrt_fusion, f32[8192]{0:T(1024)S(1)} %broadcast_multiply_fusion.1, f32[8192]{0:T(1024)S(1)} %mul.237, f32[128,128]{0,1:T(8,128)S(1)} %copy.44, ...), kind=kLoop, calls=%fused_computation.16 | loop fusion | flops 11534336 | bytes 12747264 | tf_op jit(solution)/shard_map/convert_element_type | solution.py:126
  241.4 4.1 %copy.49 = bf16[1,128,8192]{2,1,0:T(8,128)(2,1)} copy(bf16[1,128,8192]{1,2,0:T(8,128)(2,1)} %fusion.10) | data formatting | bytes 4194304 | tf_op jit(solution)/shard_map/convert_element_type | solution.py:126
  (24 shorter events, 0.1 us)
Async XLA Ops:
  6.5 19.2 %copy-start = (bf16[64,4,128]{2,1,0:T(4,128)(2,1)S(1)}, bf16[64,4,128]{2,1,0:T(4,128)(2,1)}, u32[]{:S(2)}) copy-start(bf16[64,4,128]{2,1,0:T(4,128)(2,1)} %param.14) | copy-start | bytes 196612
  6.5 52.3 %all-reduce.7.cloned.1.call-start = ((), (), s32[]{:S(2)}) async-start(), calls=%async_computation.1 | async-start | bytes 8519680 | tf_op jit(solution)/shard_map/psum | solution.py:88
  31.1 0.8 copy-start.4
  31.1 2.6 %copy-start.7 = (f32[9]{0:T(128)S(1)}, f32[9]{0:T(128)}, u32[]{:S(2)}) copy-start(f32[9]{0:T(128)} %param.23) | copy-start | bytes 112
  31.1 3.3 %copy-start.2 = (f32[7,8192]{1,0:T(8,128)S(1)}, f32[7,8192]{1,0:T(8,128)}, u32[]{:S(2)}) copy-start(f32[7,8192]{1,0:T(8,128)} %param.22) | copy-start | bytes 688132
  31.8 6.8 %copy-start.3 = (bf16[1,128,2,4,128]{4,3,2,1,0:T(4,128)(2,1)S(1)}, bf16[1,128,2,4,128]{4,3,2,1,0:T(4,128)(2,1)}, u32[]{:S(2)}) copy-start(bf16[1,128,2,4,128]{4,3,2,1,0:T(4,128)(2,1)} %param.17) | copy-start | bytes 786436
  31.9 188.1 %all-reduce.5.cloned.1.call-start = ((), (), s32[]{:S(2)}) async-start(), calls=%async_computation | async-start | bytes 8519680 | tf_op jit(solution)/shard_map/psum | solution.py:88
  61.7 12.4 %collective-permute-start.1 = (f32[128,64,128]{2,1,0:T(8,128)}, f32[128,64,128]{2,1,0:T(8,128)}, u32[]{:S(2)}, u32[]{:S(2)}) collective-permute-start(f32[128,64,128]{2,1,0:T(8,128)} %bitcast.24), channel_id=1, source_target_pairs={{0,1},{2,3},{4,5},{6,7},{8,9},{10,11},{12,13},{14,15},{16,17},{18,... | collective-permute-start | bytes 12582920 | tf_op jit(solution)/shard_map/ppermute | solution.py:106
  65.8 8.3 %collective-permute-start = (f32[128]{0:T(128)S(1)}, f32[128]{0:T(128)S(1)}, u32[]{:S(2)}, u32[]{:S(2)}) collective-permute-start(f32[128]{0:T(128)S(1)} %get-tuple-element.17), channel_id=1, source_target_pairs={{0,1},{2,3},{4,5},{6,7},{8,9},{10,11},{12,13},{14,15},{16,17},{18,... | collective-permute-start | bytes 1544 | tf_op jit(solution)/shard_map/ppermute | solution.py:106
  67.3 6.4 %copy-start.6 = (f32[128]{0:T(128)S(1)}, f32[128]{0:T(128)}, u32[]{:S(2)}) copy-start(f32[128]{0:T(128)} %param.20) | copy-start | bytes 1540
  220.0 4.7 %copy-start.1 = (f32[4,32,64,128]{3,2,1,0:T(8,128)S(1)}, f32[4,32,64,128]{3,2,1,0:T(8,128)}, u32[]{:S(2)}) copy-start(f32[4,32,64,128]{3,2,1,0:T(8,128)} %fusion.4) | copy-start | bytes 12582916
  224.7 8.2 %copy-start.5 = (f32[8192]{0:T(1024)S(1)}, f32[8192]{0:T(1024)}, u32[]{:S(2)}) copy-start(f32[8192]{0:T(1024)} %param.21) | copy-start | bytes 98308
Sparse Core Ops, SparseCore 0:
  32.0 26.8 all-reduce.6
  61.3 158.6 all-reduce.4
